TPU v7x, 32 devices: a whole 2x2x4 slice. The times are simulated.
32 devices in a mesh: branch: 2 (over x), tok: 16 (over z, y, core).
Axes of the slice: x: 2, y: 2, z: 4, core: 2. Of those that a mesh axis runs over, the one named last changes fastest.
Arguments:
- teacher_hidden: bfloat16 [2, 256, 4096], P('branch', 'tok'), may hold values from -400 to 400
- teacher_gain: float32 [2, 4096], P('branch'), may hold values from 0.5 to 1.5
- teacher_head: bfloat16 [2, 4096, 20480], P('branch', None, 'tok'), may hold values from -30 to 30
- student_hidden: bfloat16 [256, 4096], P('branch'), may hold values from -400 to 400
- student_gain: float32 [4096], replicated, may hold values from 0.5 to 1.5
- student_head: bfloat16 [4096, 20480], P('branch', 'tok'), may hold values from -30 to 30
- cluster_weights: int32 [256, 2], P(None, 'branch'), may hold values from 0 to 64, as said below
- token_ids: int32 [256], P('branch'), may hold values from 0 to 20479
Outputs:
- grad_head: float32 [4096, 20480], P('branch', 'tok')
- grad_hidden: float32 [256, 4096], P('branch', 'tok')
- grad_gain: float32 [4096], P('tok')
Inputs may be any that keep to these rules, and one draw needn't show every extreme that they name: `cluster_weights`: each token's 2 weights sum to 64.
All inputs are finite; a program needn't handle non-finite values.
Results may differ from a plain program's by a relative error of at most 0.0063.
Values may be sent and summed in bfloat16 or wider, within the bound.
No kernel may reach another device: no remote copies, remote signals or barrier semaphores. Data moves between devices by JAX's collectives and lax.ppermute only.
A program may use at most 128 MiB of HBM per device.

v0:
```python
import jax
import jax.numpy as jnp
from jax import lax
from jax.sharding import PartitionSpec as P

DEN = 64
eps = 1e-05
mix_label = 0.25
loss_scale = 64.0


def merged(value, axis, combine):
    everything = jax.tree.map(lambda part: lax.all_gather(part, axis), value)
    leading = jax.tree.map(lambda part: part[0], everything)

    def step(k, so_far):
        return combine(so_far, jax.tree.map(lambda part: part[k], everything))

    return lax.fori_loop(1, lax.axis_size(axis), step, leading)


def normalize(hidden, gain):
    values = hidden.astype(jnp.float32)
    inv_scale = lax.rsqrt(jnp.mean(values * values, axis=-1, keepdims=True) + eps)
    return ((values * inv_scale * gain).astype(jnp.bfloat16), inv_scale)


def combine_stats(first, second):
    top = jnp.maximum(first[0], second[0])
    return (top, first[1] * jnp.exp(first[0] - top) + second[1] * jnp.exp(second[0] - top))


def probabilities(logits):
    local_max = jnp.max(logits, axis=1)
    local_scaled = jnp.exp(logits - local_max[:, None])
    row_max, row_total = merged((local_max, jnp.sum(local_scaled, axis=1)), "tok", combine_stats)
    scaled = local_scaled * jnp.exp(local_max - row_max)[:, None]
    return scaled / row_total[:, None]


def per_device(
    teacher_hidden,
    teacher_gain,
    teacher_head,
    student_hidden,
    student_gain,
    student_head,
    cluster_weights,
    token_ids,
):
    rows_here = student_hidden.shape[0]
    width = student_hidden.shape[1]
    head_cols = teacher_head.shape[2]
    branch_gain = teacher_gain[0]
    branch_head = teacher_head[0]
    normed, unused_scale = normalize(
        lax.all_gather(teacher_hidden[0], "tok", axis=0, tiled=True), branch_gain
    )
    teacher_logits = jnp.dot(normed, branch_head, preferred_element_type=jnp.float32)
    weight = cluster_weights[:, 0].astype(jnp.float32) / DEN
    terms = probabilities(teacher_logits) * weight[:, None]
    mixed_all = lax.psum(terms, "branch")
    mixed = lax.dynamic_slice_in_dim(mixed_all, lax.axis_index("branch") * rows_here, rows_here, 0)
    student_normed, inv_scale = normalize(student_hidden, student_gain)
    student_logits = jnp.dot(
        student_normed,
        lax.all_gather(student_head, "branch", axis=0, tiled=True),
        preferred_element_type=jnp.float32,
    )
    student_probs = probabilities(student_logits)
    offset = lax.axis_index("tok") * head_cols
    onehot = (
        token_ids[:, None] == offset + jnp.arange(head_cols, dtype=jnp.int32)[None, :]
    ).astype(jnp.float32)
    targets = (1.0 - mix_label) * mixed + mix_label * onehot
    logit_grads = (loss_scale * (student_probs - targets)).astype(jnp.bfloat16)
    contract = (((1,), (1,)), ((), ()))
    partial_grads = lax.dot_general(
        logit_grads,
        lax.all_gather(student_head, "branch", axis=0, tiled=True),
        contract,
        preferred_element_type=jnp.float32,
    )
    normed_grads = lax.psum_scatter(partial_grads, "tok", scatter_dimension=1, tiled=True)
    slice_width = normed_grads.shape[1]
    col_start = lax.axis_index("tok") * slice_width
    hidden_cols = lax.dynamic_slice_in_dim(student_hidden, col_start, slice_width, 1).astype(
        jnp.float32
    )
    gain_cols = lax.dynamic_slice_in_dim(student_gain, col_start, slice_width, 0)
    grad_gain = lax.psum(jnp.sum(normed_grads * hidden_cols * inv_scale, axis=0), "branch")
    row_dots = lax.psum(jnp.sum(gain_cols[None, :] * normed_grads * hidden_cols, axis=1), "tok")
    grad_hidden = (
        inv_scale * gain_cols[None, :] * normed_grads
        - hidden_cols * inv_scale**3 * row_dots[:, None] / width
    )
    exchanged = lax.all_to_all(student_normed, "branch", split_axis=1, concat_axis=0, tiled=True)
    all_grads = lax.all_gather(logit_grads, "branch", axis=0, tiled=True)
    grad_head = lax.dot_general(
        exchanged, all_grads, (((0,), (0,)), ((), ())), preferred_element_type=jnp.float32
    )
    return (grad_head, grad_hidden, grad_gain)


def solution(mesh):
    in_specs = (
        P("branch", "tok", None),
        P("branch", None),
        P("branch", None, "tok"),
        P("branch", None),
        P(),
        P("branch", "tok"),
        P(None, "branch"),
        P("branch"),
    )
    out_specs = (P("branch", "tok"), P("branch", "tok"), P("tok"))
    return jax.shard_map(
        per_device, mesh=mesh, in_specs=in_specs, out_specs=out_specs, check_vma=False
    )
```

profile of v0, /device:TPU:0, one launch (start us, length us, event | category | flops | bytes accessed | tf_op | source)
XLA Modules:
  0.0 349.2 jit_solution(5427056235205396135)
XLA Ops:
  7.2 0.0 all-gather.14.cloned.1.call-start
  7.2 0.7 all-gather.14.cloned.1.call-update
  7.9 0.0 copy-start.1
  7.9 0.0 all-gather.12.cloned.1.call-start
  8.0 0.7 all-gather.12.cloned.1.call-update
  8.7 0.0 copy-start.3
  8.7 0.0 copy-start.2
  8.7 0.0 all-reduce.2.cloned.1.call-start
  8.7 0.4 copy-done.1
  9.1 0.7 copy.13
  9.8 0.6 fusion.7
  10.4 0.0 copy-done.3
  10.4 0.0 copy-start.5
  10.4 1.6 fusion.9
  12.0 42.4 %all-gather.14.cloned.1.call-done = bf16[1,256,4096]{2,1,0:T(8,128)(2,1)} async-done(((bf16[1,16,4096]{2,1,0:T(8,128)(2,1)}), bf16[1,256,4096]{2,1,0:T(8,128)(2,1)}) %all-gather.14.cloned.1.call-update) | async-done | bytes 2097168 | tf_op jit(solution)/shard_map/all_gather | solution.py:57
  54.4 2.2 fusion.4
  56.6 0.0 copy-done.5
  56.6 0.0 copy-done
  56.6 7.1 %fusion.22 = (f32[256]{0:T(256)S(1)}, f32[256,1280]{1,0:T(8,128)S(1)}) fusion(bf16[1,4096,1280]{2,1,0:T(8,128)(2,1)} %param.14, bf16[1,256,4096]{2,1,0:T(8,128)(2,1)S(1)} %copy-done, f32[4096]{0:T(1024)S(1)} %bitcast.78, f32[256]{0:T(256)S(1)} %add_rsqrt_fusion), kind=kOutput, calls=%fused_computation.50 | convolution fusion | flops 2688876288 | bytes 13912064 | tf_op jit(solution)/shard_map/dot_general | solution.py:59
  63.7 0.3 fusion.14
  64.0 19.1 %all-gather.8 = f32[16,1,256]{2,1,0:T(1,128)S(1)} all-gather(f32[1,1,256]{2,1,0:T(1,128)S(1)} %bitcast.76), channel_id=6, replica_groups=mesh['branch'=2,'tok'=16] {'tok'}, dimensions={0}, use_global_device_ids=true | all-gather | bytes 17408 | tf_op jit(solution)/shard_map/all_gather | solution.py:13
  83.1 17.4 %all-gather.7 = f32[16,1,256]{2,1,0:T(1,128)S(1)} all-gather(f32[1,1,256]{2,1,0:T(1,128)S(1)} %bitcast.71), channel_id=5, replica_groups=mesh['branch'=2,'tok'=16] {'tok'}, dimensions={0}, use_global_device_ids=true | all-gather | bytes 17408 | tf_op jit(solution)/shard_map/all_gather | solution.py:13
  100.6 0.8 while.35
  101.4 1.4 divide_multiply_fusion
  102.8 0.0 all-reduce.2.cloned.1.call-update
  102.9 0.0 copy-start.4
  102.9 0.0 reduce-scatter.2.cloned.1.call-start
  102.9 81.2 %all-gather.12.cloned.1.call-done = bf16[4096,1280]{1,0:T(8,128)(2,1)} async-done(((bf16[2048,1280]{1,0:T(8,128)(2,1)}), bf16[4096,1280]{1,0:T(8,128)(2,1)}) %all-gather.12.cloned.1.call-update) | async-done | bytes 10485776 | tf_op jit(solution)/shard_map/all_gather | solution.py:67
  184.1 6.0 %fusion.23 = (f32[128]{0:T(128)S(1)}, f32[128,1280]{1,0:T(8,128)S(1)}) fusion(bf16[128,4096]{0,1:T(8,128)(2,1)} %fusion.9, bf16[4096,1280]{1,0:T(8,128)(2,1)} %all-gather.12.cloned.1.call-done), kind=kOutput, calls=%fused_computation.51 | convolution fusion | flops 1342340992 | bytes 12190208 | tf_op jit(solution)/shard_map/dot_general | solution.py:65
  190.1 0.3 fusion.15
  190.4 21.3 %all-gather.6 = f32[16,1,128]{2,1,0:T(1,128)S(1)} all-gather(f32[1,1,128]{2,1,0:T(1,128)S(1)} %bitcast.77), channel_id=3, replica_groups=mesh['branch'=2,'tok'=16] {'tok'}, dimensions={0}, use_global_device_ids=true | all-gather | bytes 8704 | tf_op jit(solution)/shard_map/all_gather | solution.py:13
  211.7 17.4 %all-gather.5 = f32[16,1,128]{2,1,0:T(1,128)S(1)} all-gather(f32[1,1,128]{2,1,0:T(1,128)S(1)} %bitcast.74), channel_id=2, replica_groups=mesh['branch'=2,'tok'=16] {'tok'}, dimensions={0}, use_global_device_ids=true | all-gather | bytes 8704 | tf_op jit(solution)/shard_map/all_gather | solution.py:13
  229.1 0.7 while.34
  229.8 3.1 all-reduce.2.cloned.1.call-done
  232.9 1.4 multiply_convert_fusion
  234.3 8.7 %fusion.25 = f32[128,4096]{1,0:T(8,128)} fusion(bf16[128,1280]{1,0:T(8,128)(2,1)S(1)} %multiply_convert_fusion, bf16[4096,1280]{1,0:T(8,128)(2,1)} %all-gather.12.cloned.1.call-done), kind=kOutput, calls=%fused_computation.53 | convolution fusion | flops 1342177280 | bytes 12910592 | tf_op jit(solution)/shard_map/dot_general | solution.py:78
  243.0 0.0 reduce-scatter.2.cloned.1.call-update
  243.0 3.6 %all-to-all-start = ((bf16[128,2,2048]{0,2,1:T(8,128)(2,1)}), bf16[128,2,2048]{0,2,1:T(8,128)(2,1)S(1)}, u32[]{:S(2)}, u32[]{:S(2)}) async-start(bf16[128,2,2048]{0,2,1:T(8,128)(2,1)} %bitcast.4), calls=%async_computation | async-start | bytes 2097152 | tf_op jit(solution)/shard_map/all_to_all | solution.py:97
  246.6 0.1 dynamic_slice.50
  246.7 13.6 %all-to-all-done = bf16[128,2,2048]{0,2,1:T(8,128)(2,1)S(1)} async-done(((bf16[128,2,2048]{0,2,1:T(8,128)(2,1)}), bf16[128,2,2048]{0,2,1:T(8,128)(2,1)S(1)}, u32[]{:S(2)}, u32[]{:S(2)}) %all-to-all-start) | async-done | bytes 1048608 | tf_op jit(solution)/shard_map/all_to_all | solution.py:97
  260.3 0.5 copy.14
  260.9 9.1 %all_gather.44 = bf16[256,1280]{1,0:T(8,128)(2,1)S(1)} all-gather(bf16[128,1280]{1,0:T(8,128)(2,1)S(1)} %multiply_convert_fusion), channel_id=1, replica_groups=mesh['branch'=2,'tok'=16] {'branch'}, dimensions={0}, use_global_device_ids=true | all-gather | bytes 983040 | tf_op jit(solution)/shard_map/all_gather | solution.py:98
  269.9 5.7 %fusion.24 = f32[2048,1280]{1,0:T(8,128)} fusion(bf16[256,2048]{1,0:T(8,128)(2,1)S(1)} %bitcast.63, bf16[256,1280]{1,0:T(8,128)(2,1)S(1)} %all_gather.44), kind=kOutput, calls=%fused_computation.52 | convolution fusion | flops 1342177280 | bytes 12189696 | tf_op jit(solution)/shard_map/dot_general | solution.py:99
  275.6 29.3 %reduce-scatter.2.cloned.1.call-done = f32[128,256]{1,0:T(8,128)} async-done(((f32[128,4096]{1,0:T(8,128)}), f32[128,256]{1,0:T(8,128)}) %reduce-scatter.2.cloned.1.call-update) | async-done | bytes 131088 | tf_op jit(solution)/shard_map/reduce_scatter | solution.py:84
  305.0 1.0 fusion.21
  306.0 29.5 %psum.22 = f32[128]{0:T(128)S(1)} all-reduce(f32[128]{0:T(128)S(1)} %get-tuple-element.274), channel_id=1, replica_groups=mesh['branch'=2,'tok'=16] {'tok'}, use_global_device_ids=true, to_apply=%region_13.0 | all-reduce | flops 128 | bytes 1024 | tf_op jit(solution)/shard_map/psum | solution.py:92
  335.5 5.5 %psum.23 = f32[256]{0:T(256)} all-reduce(f32[256]{0:T(256)S(1)} %get-tuple-element.273), channel_id=1, replica_groups=mesh['branch'=2,'tok'=16] {'branch'}, use_global_device_ids=true, to_apply=%region_15.0 | all-reduce | flops 256 | bytes 2048 | tf_op jit(solution)/shard_map/psum | solution.py:91
  341.0 1.7 fusion.18
  (60 shorter events, 0.9 us)
Async XLA Ops:
  7.2 47.2 %all-gather.14.cloned.1.call-start = ((), (), s32[]{:S(2)}) async-start(), calls=%async_computation.5 | async-start | bytes 2228224 | tf_op jit(solution)/shard_map/all_gather | solution.py:57
  7.9 1.2 copy-start.1
  7.9 176.2 %all-gather.12.cloned.1.call-start = ((), (), s32[]{:S(2)}) async-start(), calls=%async_computation.2 | async-start | bytes 15728640 | tf_op jit(solution)/shard_map/all_gather | solution.py:67
  8.7 1.7 copy-start.3
  8.7 1.7 copy-start.2
  8.7 224.2 %all-reduce.2.cloned.1.call-start = ((), (), s32[]{:S(2)}) async-start(), calls=%async_computation.3 | async-start | bytes 2621440 | tf_op jit(solution)/shard_map/psum | solution.py:62
  10.4 46.2 %copy-start.5 = (f32[1,4096]{1,0:T(1,128)S(1)}, f32[1,4096]{1,0:T(1,128)}, u32[]{:S(2)}) copy-start(f32[1,4096]{1,0:T(1,128)} %param.13) | copy-start | bytes 49156
  54.3 2.3 copy-start
  102.9 130.0 %copy-start.4 = (s32[128]{0:T(128)S(1)}, s32[128]{0:T(128)}, u32[]{:S(2)}) copy-start(s32[128]{0:T(128)} %param.19) | copy-start | bytes 1540
  102.9 202.1 %reduce-scatter.2.cloned.1.call-start = ((), (), s32[]{:S(2)}) async-start(), calls=%async_computation.4 | async-start | bytes 2228224 | tf_op jit(solution)/shard_map/reduce_scatter | solution.py:84
  243.0 17.3 %all-to-all-start = ((bf16[128,2,2048]{0,2,1:T(8,128)(2,1)}), bf16[128,2,2048]{0,2,1:T(8,128)(2,1)S(1)}, u32[]{:S(2)}, u32[]{:S(2)}) async-start(bf16[128,2,2048]{0,2,1:T(8,128)(2,1)} %bitcast.4), calls=%async_computation | async-start | bytes 2097152 | tf_op jit(solution)/shard_map/all_to_all | solution.py:97
Sparse Core Ops, SparseCore 0:
  10.1 44.1 all-gather.13
  55.9 128.1 all-gather.11
  187.0 45.8 all-reduce.1
  243.2 61.7 reduce-scatter.1
where the time goes:
time: 350 us; the launch traced here: 349 us
  waiting for transfers between devices  171 us (49%)
  blocking collectives  119 us (34%)
  matrix products  27.5 us (8%)
  between operations  13.9 us (4%)
  other arithmetic  11.2 us (3%)
  starting transfers between devices  3.75 us (1%)
    all_gather x1, waiting for transfers between devices, per_device(): lax.all_gather(student_head, 'branch', axis=0, tiled=True)  81.2 us
    all_gather x4, blocking collectives, merged(): everything = jax.tree.map(lambda part: lax.all_gather(part, axis), value)  75.3 us
    all_gather x1, waiting for transfers between devices, per_device(): lax.all_gather(teacher_hidden[0], 'tok', axis=0, tiled=True)  42.4 us
    psum x1, blocking collectives, per_device(): lax.psum(jnp.sum(gain_cols[None, :] * normed_grads * hidden_cols, axis=1)...  29.5 us
    reduce_scatter x1, waiting for transfers between devices, per_device(): lax.psum_scatter(partial_grads, 'tok', scatter_dimension=1, tiled=True)  29.3 us
    all_to_all x1, waiting for transfers between devices, per_device(): lax.all_to_all(student_normed, 'branch', split_axis=1, concat_axis=0, til...  13.6 us
    all_gather x1, blocking collectives, per_device(): all_grads = lax.all_gather(logit_grads, 'branch', axis=0, tiled=True)  9.09 us
    dot_general x1, matrix products, per_device(): lax.dot_general(logit_grads, lax.all_gather(student_head, 'branch', axis=...  8.73 us
  transfers between devices with their start and end apart: 5, of which 5 were waited for; matrix products, arithmetic and copies ran while one was open for 8% of the time, Pallas kernels for 0%

commit v1 on v0

--- a/solution.py
+++ b/solution.py
@@ -7,6 +7,18 @@
 eps = 1e-05
 mix_label = 0.25
 loss_scale = 64.0
+
+
+def collect(array, axis, dim):
+    ways, here, step = (lax.axis_size(axis), lax.axis_index(axis), array.shape[dim])
+    shape = [n * ways if d == dim else n for d, n in enumerate(array.shape)]
+    full = lax.dynamic_update_slice_in_dim(
+        jnp.zeros(shape, array.dtype), array, here * step, axis=dim
+    )
+    for far in range(1, ways):
+        array = lax.ppermute(array, axis, [(d, (d + 1) % ways) for d in range(ways)])
+        full = lax.dynamic_update_slice_in_dim(full, array, (here - far) % ways * step, axis=dim)
+    return full
 
 
 def merged(value, axis, combine):
@@ -53,9 +65,7 @@
     head_cols = teacher_head.shape[2]
     branch_gain = teacher_gain[0]
     branch_head = teacher_head[0]
-    normed, unused_scale = normalize(
-        lax.all_gather(teacher_hidden[0], "tok", axis=0, tiled=True), branch_gain
-    )
+    normed, unused_scale = normalize(collect(teacher_hidden[0], "tok", 0), branch_gain)
     teacher_logits = jnp.dot(normed, branch_head, preferred_element_type=jnp.float32)
     weight = cluster_weights[:, 0].astype(jnp.float32) / DEN
     terms = probabilities(teacher_logits) * weight[:, None]

time: 350 us -> 322 us (0.920)
  waiting for transfers between devices: 171 us -> 145 us
    ppermute x0 -> x15, waiting for transfers between devices: none -> 103 us  [collect(): lax.ppermute(array, axis, [(d, (d + 1) % ways) for d in range(ways)])]
    all_gather x1, waiting for transfers between devices: 81.2 us -> 0.02 us  [per_device(): lax.all_gather(student_head, 'branch', axis=0, tiled=True)]
    all_gather x1 -> x0, waiting for transfers between devices: 42.4 us -> none  [per_device(): lax.all_gather(teacher_hidden[0], 'tok', axis=0, tiled=True)]
  transfers between devices with their start and end apart: 5 -> 19, of which waited for: 5 -> 17; matrix products, arithmetic and copies ran while one was open for 8% -> 8% of each run, Pallas kernels for 0% -> 0%
where the time goes in v1:
time: 322 us; the launch traced here: 321 us
  waiting for transfers between devices  145 us (45%)
  blocking collectives  117 us (36%)
  matrix products  27.8 us (9%)
  between operations  14 us (4%)
  other arithmetic  9.47 us (3%)
  starting transfers between devices  4.29 us (1%)
    ppermute x15, waiting for transfers between devices, collect(): lax.ppermute(array, axis, [(d, (d + 1) % ways) for d in range(ways)])  103 us
    all_gather x4, blocking collectives, merged(): everything = jax.tree.map(lambda part: lax.all_gather(part, axis), value)  72.5 us
    psum x1, blocking collectives, per_device(): lax.psum(jnp.sum(gain_cols[None, :] * normed_grads * hidden_cols, axis=1)...  29.5 us
    reduce_scatter x1, waiting for transfers between devices, per_device(): lax.psum_scatter(partial_grads, 'tok', scatter_dimension=1, tiled=True)  27.6 us
    all_to_all x1, waiting for transfers between devices, per_device(): lax.all_to_all(student_normed, 'branch', split_axis=1, concat_axis=0, til...  14.5 us
    all_gather x1, blocking collectives, per_device(): all_grads = lax.all_gather(logit_grads, 'branch', axis=0, tiled=True)  9.95 us
    dot_general x1, matrix products, per_device(): lax.dot_general(logit_grads, lax.all_gather(student_head, 'branch', axis=...  8.75 us
    dot_general x1, matrix products, per_device(): jnp.dot(normed, branch_head, preferred_element_type=jnp.float32)  6.99 us
  transfers between devices with their start and end apart: 19, of which 17 were waited for; matrix products, arithmetic and copies ran while one was open for 8% of the time, Pallas kernels for 0%

profile of v1, /device:TPU:0, one launch (start us, length us, event | category | flops | bytes accessed | tf_op | source)
XLA Modules:
  0.0 321.3 jit_solution(14869688313189223548)
XLA Ops:
  7.2 0.5 collective-permute-start
  7.8 0.1 all-gather.10.cloned.1.call-update
  8.0 0.5 copy-done
  8.4 0.7 copy.13
  9.1 0.6 fusion.7
  9.7 0.2 broadcast_in_dim.2
  9.9 0.1 copy-done.1
  10.0 1.5 fusion.9
  11.6 4.0 %collective-permute-done = bf16[16,4096]{1,0:T(8,128)(2,1)S(1)} collective-permute-done((bf16[16,4096]{1,0:T(8,128)(2,1)}, bf16[16,4096]{1,0:T(8,128)(2,1)S(1)}, u32[]{:S(2)}, u32[]{:S(2)}) %collective-permute-start) | collective-permute-done | bytes 131104 | tf_op jit(solution)/shard_map/ppermute | solution.py:19
  15.6 7.1 %collective-permute-done.1 = bf16[16,4096]{1,0:T(8,128)(2,1)S(1)} collective-permute-done((bf16[16,4096]{1,0:T(8,128)(2,1)S(1)}, bf16[16,4096]{1,0:T(8,128)(2,1)S(1)}, u32[]{:S(2)}, u32[]{:S(2)}) %collective-permute-start.1) | collective-permute-done | bytes 131104 | tf_op jit(solution)/shard_map/ppermute | solution.py:19
  22.7 7.1 %collective-permute-done.2 = bf16[16,4096]{1,0:T(8,128)(2,1)S(1)} collective-permute-done((bf16[16,4096]{1,0:T(8,128)(2,1)S(1)}, bf16[16,4096]{1,0:T(8,128)(2,1)S(1)}, u32[]{:S(2)}, u32[]{:S(2)}) %collective-permute-start.2) | collective-permute-done | bytes 131104 | tf_op jit(solution)/shard_map/ppermute | solution.py:19
  29.8 7.1 %collective-permute-done.3 = bf16[16,4096]{1,0:T(8,128)(2,1)S(1)} collective-permute-done((bf16[16,4096]{1,0:T(8,128)(2,1)S(1)}, bf16[16,4096]{1,0:T(8,128)(2,1)S(1)}, u32[]{:S(2)}, u32[]{:S(2)}) %collective-permute-start.3) | collective-permute-done | bytes 131104 | tf_op jit(solution)/shard_map/ppermute | solution.py:19
  36.9 7.1 %collective-permute-done.4 = bf16[16,4096]{1,0:T(8,128)(2,1)S(1)} collective-permute-done((bf16[16,4096]{1,0:T(8,128)(2,1)S(1)}, bf16[16,4096]{1,0:T(8,128)(2,1)S(1)}, u32[]{:S(2)}, u32[]{:S(2)}) %collective-permute-start.4) | collective-permute-done | bytes 131104 | tf_op jit(solution)/shard_map/ppermute | solution.py:19
  44.0 7.1 %collective-permute-done.5 = bf16[16,4096]{1,0:T(8,128)(2,1)S(1)} collective-permute-done((bf16[16,4096]{1,0:T(8,128)(2,1)S(1)}, bf16[16,4096]{1,0:T(8,128)(2,1)S(1)}, u32[]{:S(2)}, u32[]{:S(2)}) %collective-permute-start.5) | collective-permute-done | bytes 131104 | tf_op jit(solution)/shard_map/ppermute | solution.py:19
  51.1 7.1 %collective-permute-done.6 = bf16[16,4096]{1,0:T(8,128)(2,1)S(1)} collective-permute-done((bf16[16,4096]{1,0:T(8,128)(2,1)S(1)}, bf16[16,4096]{1,0:T(8,128)(2,1)S(1)}, u32[]{:S(2)}, u32[]{:S(2)}) %collective-permute-start.6) | collective-permute-done | bytes 131104 | tf_op jit(solution)/shard_map/ppermute | solution.py:19
  58.2 7.1 %collective-permute-done.7 = bf16[16,4096]{1,0:T(8,128)(2,1)S(1)} collective-permute-done((bf16[16,4096]{1,0:T(8,128)(2,1)S(1)}, bf16[16,4096]{1,0:T(8,128)(2,1)S(1)}, u32[]{:S(2)}, u32[]{:S(2)}) %collective-permute-start.7) | collective-permute-done | bytes 131104 | tf_op jit(solution)/shard_map/ppermute | solution.py:19
  65.3 7.1 %collective-permute-done.8 = bf16[16,4096]{1,0:T(8,128)(2,1)S(1)} collective-permute-done((bf16[16,4096]{1,0:T(8,128)(2,1)S(1)}, bf16[16,4096]{1,0:T(8,128)(2,1)S(1)}, u32[]{:S(2)}, u32[]{:S(2)}) %collective-permute-start.8) | collective-permute-done | bytes 131104 | tf_op jit(solution)/shard_map/ppermute | solution.py:19
  72.4 7.1 %collective-permute-done.9 = bf16[16,4096]{1,0:T(8,128)(2,1)S(1)} collective-permute-done((bf16[16,4096]{1,0:T(8,128)(2,1)S(1)}, bf16[16,4096]{1,0:T(8,128)(2,1)S(1)}, u32[]{:S(2)}, u32[]{:S(2)}) %collective-permute-start.9) | collective-permute-done | bytes 131104 | tf_op jit(solution)/shard_map/ppermute | solution.py:19
  79.4 7.1 %collective-permute-done.10 = bf16[16,4096]{1,0:T(8,128)(2,1)S(1)} collective-permute-done((bf16[16,4096]{1,0:T(8,128)(2,1)S(1)}, bf16[16,4096]{1,0:T(8,128)(2,1)S(1)}, u32[]{:S(2)}, u32[]{:S(2)}) %collective-permute-start.10) | collective-permute-done | bytes 131104 | tf_op jit(solution)/shard_map/ppermute | solution.py:19
  86.5 7.1 %collective-permute-done.11 = bf16[16,4096]{1,0:T(8,128)(2,1)S(1)} collective-permute-done((bf16[16,4096]{1,0:T(8,128)(2,1)S(1)}, bf16[16,4096]{1,0:T(8,128)(2,1)S(1)}, u32[]{:S(2)}, u32[]{:S(2)}) %collective-permute-start.11) | collective-permute-done | bytes 131104 | tf_op jit(solution)/shard_map/ppermute | solution.py:19
  93.6 7.1 %collective-permute-done.12 = bf16[16,4096]{1,0:T(8,128)(2,1)S(1)} collective-permute-done((bf16[16,4096]{1,0:T(8,128)(2,1)S(1)}, bf16[16,4096]{1,0:T(8,128)(2,1)S(1)}, u32[]{:S(2)}, u32[]{:S(2)}) %collective-permute-start.12) | collective-permute-done | bytes 131104 | tf_op jit(solution)/shard_map/ppermute | solution.py:19
  100.7 7.1 %collective-permute-done.13 = bf16[16,4096]{1,0:T(8,128)(2,1)S(1)} collective-permute-done((bf16[16,4096]{1,0:T(8,128)(2,1)S(1)}, bf16[16,4096]{1,0:T(8,128)(2,1)S(1)}, u32[]{:S(2)}, u32[]{:S(2)}) %collective-permute-start.13) | collective-permute-done | bytes 131104 | tf_op jit(solution)/shard_map/ppermute | solution.py:19
  107.8 7.1 %collective-permute-done.14 = bf16[16,4096]{1,0:T(8,128)(2,1)S(1)} collective-permute-done((bf16[16,4096]{1,0:T(8,128)(2,1)S(1)}, bf16[16,4096]{1,0:T(8,128)(2,1)S(1)}, u32[]{:S(2)}, u32[]{:S(2)}) %collective-permute-start.14) | collective-permute-done | bytes 131104 | tf_op jit(solution)/shard_map/ppermute | solution.py:19
  114.9 0.5 fusion.4
  115.4 7.0 %fusion.21 = (f32[256]{0:T(256)S(1)}, f32[256,1280]{1,0:T(8,128)S(1)}) fusion(bf16[1,4096,1280]{2,1,0:T(8,128)(2,1)} %param.14, bf16[256,4096]{1,0:T(8,128)(2,1)S(1)} %constant_dynamic-update-slice_fusion, f32[4096]{0:T(1024)S(1)} %bitcast.72, f32[256]{0:T(256)S(1)} %add_rsqrt_fusion), kind=kOutput, calls=%fused_computation.65 | convolution fusion | flops 2688876288 | bytes 13912064 | tf_op jit(solution)/shard_map/dot_general | solution.py:69
  122.4 0.3 fusion.13
  122.7 17.2 %all-gather.7 = f32[16,1,256]{2,1,0:T(1,128)S(1)} all-gather(f32[1,1,256]{2,1,0:T(1,128)S(1)} %bitcast.70), channel_id=5, replica_groups=mesh['branch'=2,'tok'=16] {'tok'}, dimensions={0}, use_global_device_ids=true | all-gather | bytes 17408 | tf_op jit(solution)/shard_map/all_gather | solution.py:25
  139.9 19.1 %all-gather.6 = f32[16,1,256]{2,1,0:T(1,128)S(1)} all-gather(f32[1,1,256]{2,1,0:T(1,128)S(1)} %bitcast.65), channel_id=4, replica_groups=mesh['branch'=2,'tok'=16] {'tok'}, dimensions={0}, use_global_device_ids=true | all-gather | bytes 17408 | tf_op jit(solution)/shard_map/all_gather | solution.py:25
  159.0 0.8 while.35
  159.9 1.4 divide_multiply_fusion
  161.4 6.4 %fusion.22 = (f32[128]{0:T(128)S(1)}, f32[128,1280]{1,0:T(8,128)S(1)}) fusion(bf16[128,4096]{0,1:T(8,128)(2,1)} %fusion.9, bf16[4096,1280]{1,0:T(8,128)(2,1)} %all-gather.10.cloned.1.call-done), kind=kOutput, calls=%fused_computation.66 | convolution fusion | flops 1342340992 | bytes 12190208 | tf_op jit(solution)/shard_map/dot_general | solution.py:75
  167.8 0.3 fusion.14
  168.1 17.4 %all-gather.5 = f32[16,1,128]{2,1,0:T(1,128)S(1)} all-gather(f32[1,1,128]{2,1,0:T(1,128)S(1)} %bitcast.71), channel_id=3, replica_groups=mesh['branch'=2,'tok'=16] {'tok'}, dimensions={0}, use_global_device_ids=true | all-gather | bytes 8704 | tf_op jit(solution)/shard_map/all_gather | solution.py:25
  185.5 18.8 %all-gather.4 = f32[16,1,128]{2,1,0:T(1,128)S(1)} all-gather(f32[1,1,128]{2,1,0:T(1,128)S(1)} %bitcast.68), channel_id=2, replica_groups=mesh['branch'=2,'tok'=16] {'tok'}, dimensions={0}, use_global_device_ids=true | all-gather | bytes 8704 | tf_op jit(solution)/shard_map/all_gather | solution.py:25
  204.3 0.7 while.34
  205.0 1.4 multiply_convert_fusion
  206.4 8.8 %fusion.24 = f32[128,4096]{1,0:T(8,128)} fusion(bf16[128,1280]{1,0:T(8,128)(2,1)S(1)} %multiply_convert_fusion, bf16[4096,1280]{1,0:T(8,128)(2,1)} %all-gather.10.cloned.1.call-done), kind=kOutput, calls=%fused_computation.68 | convolution fusion | flops 1342177280 | bytes 12910592 | tf_op jit(solution)/shard_map/dot_general | solution.py:88
  215.2 3.6 %all-to-all-start = ((bf16[128,2,2048]{0,2,1:T(8,128)(2,1)}), bf16[128,2,2048]{0,2,1:T(8,128)(2,1)S(1)}, u32[]{:S(2)}, u32[]{:S(2)}) async-start(bf16[128,2,2048]{0,2,1:T(8,128)(2,1)} %bitcast.4), calls=%async_computation | async-start | bytes 2097152 | tf_op jit(solution)/shard_map/all_to_all | solution.py:107
  218.8 0.1 dynamic_slice.50
  218.9 14.5 %all-to-all-done = bf16[128,2,2048]{0,2,1:T(8,128)(2,1)S(1)} async-done(((bf16[128,2,2048]{0,2,1:T(8,128)(2,1)}), bf16[128,2,2048]{0,2,1:T(8,128)(2,1)S(1)}, u32[]{:S(2)}, u32[]{:S(2)}) %all-to-all-start) | async-done | bytes 1048608 | tf_op jit(solution)/shard_map/all_to_all | solution.py:107
  233.3 0.5 copy.14
  233.9 9.9 %all_gather.40 = bf16[256,1280]{1,0:T(8,128)(2,1)S(1)} all-gather(bf16[128,1280]{1,0:T(8,128)(2,1)S(1)} %multiply_convert_fusion), channel_id=1, replica_groups=mesh['branch'=2,'tok'=16] {'branch'}, dimensions={0}, use_global_device_ids=true | all-gather | bytes 983040 | tf_op jit(solution)/shard_map/all_gather | solution.py:108
  243.8 5.7 %fusion.23 = f32[2048,1280]{1,0:T(8,128)} fusion(bf16[256,2048]{1,0:T(8,128)(2,1)S(1)} %bitcast.56, bf16[256,1280]{1,0:T(8,128)(2,1)S(1)} %all_gather.40), kind=kOutput, calls=%fused_computation.67 | convolution fusion | flops 1342177280 | bytes 12189696 | tf_op jit(solution)/shard_map/dot_general | solution.py:109
  249.5 27.6 %reduce-scatter.2.cloned.1.call-done = f32[128,256]{1,0:T(8,128)} async-done(((f32[128,4096]{1,0:T(8,128)}), f32[128,256]{1,0:T(8,128)}) %reduce-scatter.2.cloned.1.call-update) | async-done | bytes 131088 | tf_op jit(solution)/shard_map/reduce_scatter | solution.py:94
  277.1 1.0 fusion.20
  278.2 29.5 %psum.22 = f32[128]{0:T(128)S(1)} all-reduce(f32[128]{0:T(128)S(1)} %get-tuple-element.274), channel_id=1, replica_groups=mesh['branch'=2,'tok'=16] {'tok'}, use_global_device_ids=true, to_apply=%region_13.14 | all-reduce | flops 128 | bytes 1024 | tf_op jit(solution)/shard_map/psum | solution.py:102
  307.7 5.5 %psum.23 = f32[256]{0:T(256)} all-reduce(f32[256]{0:T(256)S(1)} %get-tuple-element.273), channel_id=1, replica_groups=mesh['branch'=2,'tok'=16] {'branch'}, use_global_device_ids=true, to_apply=%region_15.16 | all-reduce | flops 256 | bytes 2048 | tf_op jit(solution)/shard_map/psum | solution.py:101
  313.1 1.7 fusion.17
  (104 shorter events, 1.4 us)
Async XLA Ops:
  7.2 154.2 %all-gather.10.cloned.1.call-start = ((), (), s32[]{:S(2)}) async-start(), calls=%async_computation.2 | async-start | bytes 15728640 | tf_op jit(solution)/shard_map/all_gather | solution.py:77
  7.2 1.2 copy-start
  7.2 8.4 %collective-permute-start = (bf16[16,4096]{1,0:T(8,128)(2,1)}, bf16[16,4096]{1,0:T(8,128)(2,1)S(1)}, u32[]{:S(2)}, u32[]{:S(2)}) collective-permute-start(bf16[16,4096]{1,0:T(8,128)(2,1)} %bitcast.58), channel_id=1, source_target_pairs={{0,1},{1,2},{2,3},{3,4},{4,5},{5,6},{6,7},{7,8},{8,9},{9,10},{10,1... | collective-permute-start | bytes 393224 | tf_op jit(solution)/shard_map/ppermute | solution.py:19
  7.9 197.1 %all-reduce.2.cloned.1.call-start = ((), (), s32[]{:S(2)}) async-start(), calls=%async_computation.3 | async-start | bytes 2621440 | tf_op jit(solution)/shard_map/psum | solution.py:72
  9.1 0.9 copy-start.1
  9.1 0.9 copy-start.2
  9.7 1.9 copy-start.3
  15.6 7.1 %collective-permute-start.1 = (bf16[16,4096]{1,0:T(8,128)(2,1)S(1)}, bf16[16,4096]{1,0:T(8,128)(2,1)S(1)}, u32[]{:S(2)}, u32[]{:S(2)}) collective-permute-start(bf16[16,4096]{1,0:T(8,128)(2,1)S(1)} %collective-permute-done), channel_id=1, source_target_pairs={{0,1},{1,2},{2,3},{3,4},{4,5},{5,6},{6,7},{7,8},{8,9},{9,10},{10,1... | collective-permute-start | bytes 393224 | tf_op jit(solution)/shard_map/ppermute | solution.py:19
  22.7 7.1 %collective-permute-start.2 = (bf16[16,4096]{1,0:T(8,128)(2,1)S(1)}, bf16[16,4096]{1,0:T(8,128)(2,1)S(1)}, u32[]{:S(2)}, u32[]{:S(2)}) collective-permute-start(bf16[16,4096]{1,0:T(8,128)(2,1)S(1)} %collective-permute-done.1), channel_id=1, source_target_pairs={{0,1},{1,2},{2,3},{3,4},{4,5},{5,6},{6,7},{7,8},{8,9},{9,10},{10,1... | collective-permute-start | bytes 393224 | tf_op jit(solution)/shard_map/ppermute | solution.py:19
  29.8 7.1 %collective-permute-start.3 = (bf16[16,4096]{1,0:T(8,128)(2,1)S(1)}, bf16[16,4096]{1,0:T(8,128)(2,1)S(1)}, u32[]{:S(2)}, u32[]{:S(2)}) collective-permute-start(bf16[16,4096]{1,0:T(8,128)(2,1)S(1)} %collective-permute-done.2), channel_id=1, source_target_pairs={{0,1},{1,2},{2,3},{3,4},{4,5},{5,6},{6,7},{7,8},{8,9},{9,10},{10,1... | collective-permute-start | bytes 393224 | tf_op jit(solution)/shard_map/ppermute | solution.py:19
  36.9 7.1 %collective-permute-start.4 = (bf16[16,4096]{1,0:T(8,128)(2,1)S(1)}, bf16[16,4096]{1,0:T(8,128)(2,1)S(1)}, u32[]{:S(2)}, u32[]{:S(2)}) collective-permute-start(bf16[16,4096]{1,0:T(8,128)(2,1)S(1)} %collective-permute-done.3), channel_id=1, source_target_pairs={{0,1},{1,2},{2,3},{3,4},{4,5},{5,6},{6,7},{7,8},{8,9},{9,10},{10,1... | collective-permute-start | bytes 393224 | tf_op jit(solution)/shard_map/ppermute | solution.py:19
  44.0 7.1 %collective-permute-start.5 = (bf16[16,4096]{1,0:T(8,128)(2,1)S(1)}, bf16[16,4096]{1,0:T(8,128)(2,1)S(1)}, u32[]{:S(2)}, u32[]{:S(2)}) collective-permute-start(bf16[16,4096]{1,0:T(8,128)(2,1)S(1)} %collective-permute-done.4), channel_id=1, source_target_pairs={{0,1},{1,2},{2,3},{3,4},{4,5},{5,6},{6,7},{7,8},{8,9},{9,10},{10,1... | collective-permute-start | bytes 393224 | tf_op jit(solution)/shard_map/ppermute | solution.py:19
  51.1 7.1 %collective-permute-start.6 = (bf16[16,4096]{1,0:T(8,128)(2,1)S(1)}, bf16[16,4096]{1,0:T(8,128)(2,1)S(1)}, u32[]{:S(2)}, u32[]{:S(2)}) collective-permute-start(bf16[16,4096]{1,0:T(8,128)(2,1)S(1)} %collective-permute-done.5), channel_id=1, source_target_pairs={{0,1},{1,2},{2,3},{3,4},{4,5},{5,6},{6,7},{7,8},{8,9},{9,10},{10,1... | collective-permute-start | bytes 393224 | tf_op jit(solution)/shard_map/ppermute | solution.py:19
  58.2 7.1 %collective-permute-start.7 = (bf16[16,4096]{1,0:T(8,128)(2,1)S(1)}, bf16[16,4096]{1,0:T(8,128)(2,1)S(1)}, u32[]{:S(2)}, u32[]{:S(2)}) collective-permute-start(bf16[16,4096]{1,0:T(8,128)(2,1)S(1)} %collective-permute-done.6), channel_id=1, source_target_pairs={{0,1},{1,2},{2,3},{3,4},{4,5},{5,6},{6,7},{7,8},{8,9},{9,10},{10,1... | collective-permute-start | bytes 393224 | tf_op jit(solution)/shard_map/ppermute | solution.py:19
  58.2 57.2 %copy-start.5 = (f32[1,4096]{1,0:T(1,128)S(1)}, f32[1,4096]{1,0:T(1,128)}, u32[]{:S(2)}) copy-start(f32[1,4096]{1,0:T(1,128)} %param.13) | copy-start | bytes 49156
  65.2 7.1 %collective-permute-start.8 = (bf16[16,4096]{1,0:T(8,128)(2,1)S(1)}, bf16[16,4096]{1,0:T(8,128)(2,1)S(1)}, u32[]{:S(2)}, u32[]{:S(2)}) collective-permute-start(bf16[16,4096]{1,0:T(8,128)(2,1)S(1)} %collective-permute-done.7), channel_id=1, source_target_pairs={{0,1},{1,2},{2,3},{3,4},{4,5},{5,6},{6,7},{7,8},{8,9},{9,10},{10,1... | collective-permute-start | bytes 393224 | tf_op jit(solution)/shard_map/ppermute | solution.py:19
  72.3 7.1 %collective-permute-start.9 = (bf16[16,4096]{1,0:T(8,128)(2,1)S(1)}, bf16[16,4096]{1,0:T(8,128)(2,1)S(1)}, u32[]{:S(2)}, u32[]{:S(2)}) collective-permute-start(bf16[16,4096]{1,0:T(8,128)(2,1)S(1)} %collective-permute-done.8), channel_id=1, source_target_pairs={{0,1},{1,2},{2,3},{3,4},{4,5},{5,6},{6,7},{7,8},{8,9},{9,10},{10,1... | collective-permute-start | bytes 393224 | tf_op jit(solution)/shard_map/ppermute | solution.py:19
  79.4 7.1 %collective-permute-start.10 = (bf16[16,4096]{1,0:T(8,128)(2,1)S(1)}, bf16[16,4096]{1,0:T(8,128)(2,1)S(1)}, u32[]{:S(2)}, u32[]{:S(2)}) collective-permute-start(bf16[16,4096]{1,0:T(8,128)(2,1)S(1)} %collective-permute-done.9), channel_id=1, source_target_pairs={{0,1},{1,2},{2,3},{3,4},{4,5},{5,6},{6,7},{7,8},{8,9},{9,10},{10,1... | collective-permute-start | bytes 393224 | tf_op jit(solution)/shard_map/ppermute | solution.py:19
  86.5 7.1 %collective-permute-start.11 = (bf16[16,4096]{1,0:T(8,128)(2,1)S(1)}, bf16[16,4096]{1,0:T(8,128)(2,1)S(1)}, u32[]{:S(2)}, u32[]{:S(2)}) collective-permute-start(bf16[16,4096]{1,0:T(8,128)(2,1)S(1)} %collective-permute-done.10), channel_id=1, source_target_pairs={{0,1},{1,2},{2,3},{3,4},{4,5},{5,6},{6,7},{7,8},{8,9},{9,10},{10,1... | collective-permute-start | bytes 393224 | tf_op jit(solution)/shard_map/ppermute | solution.py:19
  93.6 7.1 %collective-permute-start.12 = (bf16[16,4096]{1,0:T(8,128)(2,1)S(1)}, bf16[16,4096]{1,0:T(8,128)(2,1)S(1)}, u32[]{:S(2)}, u32[]{:S(2)}) collective-permute-start(bf16[16,4096]{1,0:T(8,128)(2,1)S(1)} %collective-permute-done.11), channel_id=1, source_target_pairs={{0,1},{1,2},{2,3},{3,4},{4,5},{5,6},{6,7},{7,8},{8,9},{9,10},{10,1... | collective-permute-start | bytes 393224 | tf_op jit(solution)/shard_map/ppermute | solution.py:19
  100.7 7.1 %collective-permute-start.13 = (bf16[16,4096]{1,0:T(8,128)(2,1)S(1)}, bf16[16,4096]{1,0:T(8,128)(2,1)S(1)}, u32[]{:S(2)}, u32[]{:S(2)}) collective-permute-start(bf16[16,4096]{1,0:T(8,128)(2,1)S(1)} %collective-permute-done.12), channel_id=1, source_target_pairs={{0,1},{1,2},{2,3},{3,4},{4,5},{5,6},{6,7},{7,8},{8,9},{9,10},{10,1... | collective-permute-start | bytes 393224 | tf_op jit(solution)/shard_map/ppermute | solution.py:19
  107.8 7.1 %collective-permute-start.14 = (bf16[16,4096]{1,0:T(8,128)(2,1)S(1)}, bf16[16,4096]{1,0:T(8,128)(2,1)S(1)}, u32[]{:S(2)}, u32[]{:S(2)}) collective-permute-start(bf16[16,4096]{1,0:T(8,128)(2,1)S(1)} %collective-permute-done.13), channel_id=1, source_target_pairs={{0,1},{1,2},{2,3},{3,4},{4,5},{5,6},{6,7},{7,8},{8,9},{9,10},{10,1... | collective-permute-start | bytes 393224 | tf_op jit(solution)/shard_map/ppermute | solution.py:19
  161.3 43.7 %copy-start.4 = (s32[128]{0:T(128)S(1)}, s32[128]{0:T(128)}, u32[]{:S(2)}) copy-start(s32[128]{0:T(128)} %param.19) | copy-start | bytes 1540
  161.3 115.8 %reduce-scatter.2.cloned.1.call-start = ((), (), s32[]{:S(2)}) async-start(), calls=%async_computation.4 | async-start | bytes 2228224 | tf_op jit(solution)/shard_map/reduce_scatter | solution.py:94
  215.2 18.1 %all-to-all-start = ((bf16[128,2,2048]{0,2,1:T(8,128)(2,1)}), bf16[128,2,2048]{0,2,1:T(8,128)(2,1)S(1)}, u32[]{:S(2)}, u32[]{:S(2)}) async-start(bf16[128,2,2048]{0,2,1:T(8,128)(2,1)} %bitcast.4), calls=%async_computation | async-start | bytes 2097152 | tf_op jit(solution)/shard_map/all_to_all | solution.py:107
Sparse Core Ops, SparseCore 0:
  9.5 132.1 all-gather.9
  161.4 43.5 all-reduce.1
  215.3 61.7 reduce-scatter.1
